TPU v7x, 32 devices: a whole 2x2x4 slice. The times are simulated.
32 devices in a mesh: row: 2 (over x), col: 16 (over z, y, core).
Axes of the slice: x: 2, y: 2, z: 4, core: 2. Of those that a mesh axis runs over, the one named last changes fastest.
Arguments:
- features: bfloat16 [64, 768, 256], P('row', 'col'), may hold values from -6 to 6
- conv_one: bfloat16 [3, 3, 256, 256], replicated, may hold values from -0.125 to 0.125
- bias_one: float32 [256], replicated, may hold values from -3 to 3
- conv_two: bfloat16 [3, 3, 256, 512], replicated, may hold values from -0.125 to 0.125
- bias_two: float32 [512], replicated, may hold values from -3 to 3
- conv_three: bfloat16 [16, 3, 3, 32, 32], P('col'), may hold values from -0.375 to 0.375
- bias_three: float32 [512], P('col'), may hold values from -3 to 3
Outputs:
- encoded: bfloat16 [32, 512, 384], P('row', 'col')
All inputs are finite; a program needn't handle non-finite values.
Results may differ from a plain program's by a relative error of at most 0.0051.
Values may be sent and summed in bfloat16 or wider, within the bound.
A program may use at most 64 MiB of HBM per device.

v0:
```python
import jax
import jax.numpy as jnp
from jax import lax
from jax.sharding import PartitionSpec as P


def padded_2(block, sides, width):
    for axis, dim in sides:
        count = lax.axis_size(axis)
        forward = [(i, i + 1) for i in range(count - 1)]
        backward = [(target, source) for source, target in forward]
        low = lax.ppermute(
            lax.slice_in_dim(block, block.shape[dim] - width, None, axis=dim), axis, forward
        )
        high = lax.ppermute(lax.slice_in_dim(block, 0, width, axis=dim), axis, backward)
        block = jnp.concatenate([low, block, high], axis=dim)
    return block


def passed_along(block, axis, distance):
    devices = range(lax.axis_size(axis))
    route = [(i - distance, i) for i in devices if i - distance in devices]
    return lax.ppermute(block, axis, route)


def conv_taps(padded, weight, out_rows, out_cols, stride):
    summed = None
    for tap_row in range(3):
        for tap_col in range(3):
            window = lax.slice(
                padded,
                (tap_row, tap_col, 0),
                (
                    tap_row + stride * (out_rows - 1) + 1,
                    tap_col + stride * (out_cols - 1) + 1,
                    padded.shape[2],
                ),
                (stride, stride, 1),
            )
            product = jnp.dot(
                window.reshape(out_rows * out_cols, padded.shape[2]),
                weight[tap_row, tap_col],
                preferred_element_type=jnp.float32,
            )
            summed = product if summed is None else summed + product
    return summed.reshape(out_rows, out_cols, weight.shape[3])


def on_device(features, conv_one, bias_one, conv_two, bias_two, conv_three, bias_three):
    tile_rows = features.shape[0]
    tile_cols = features.shape[1]
    padded = padded_2(features, (("row", 0), ("col", 1)), 1)
    summed = conv_taps(padded, conv_one, tile_rows, tile_cols, 1)
    layer_one = jax.nn.relu(summed + bias_one).astype(jnp.bfloat16)
    upper_row = passed_along(layer_one[tile_rows - 1 :], "row", 1)
    extended = jnp.concatenate([upper_row, layer_one], 0)
    left_column = passed_along(extended[:, tile_cols - 1 :], "col", 1)
    extended = jnp.concatenate([left_column, extended], 1)
    summed = conv_taps(extended, conv_two, tile_rows // 2, tile_cols // 2, 2)
    layer_two = jax.nn.relu(summed + bias_two).astype(jnp.bfloat16)
    grouped = lax.all_to_all(layer_two, "col", split_axis=2, concat_axis=1, tiled=True)
    grouped = padded_2(grouped, (("row", 0),), 1)
    grouped = jnp.pad(grouped, ((0, 0), (1, 1), (0, 0)))
    local_groups = conv_three.shape[0]
    group_width = conv_three.shape[3]
    out_rows = layer_two.shape[0]
    full_cols = grouped.shape[1] - 2
    summed = None
    for tap_row in range(3):
        for tap_col in range(3):
            window = grouped[tap_row : tap_row + out_rows, tap_col : tap_col + full_cols].reshape(
                out_rows, full_cols, local_groups, group_width
            )
            product = jnp.einsum(
                "rwgi,gio->rgow",
                window,
                conv_three[:, tap_row, tap_col],
                preferred_element_type=jnp.float32,
            )
            summed = product if summed is None else summed + product
    result = (
        summed.reshape(out_rows, local_groups * group_width, full_cols) + bias_three[None, :, None]
    )
    return result.astype(jnp.bfloat16)


def solution(mesh):
    in_specs = (
        P("row", "col", None),
        P(),
        P(),
        P(),
        P(),
        P("col", None, None, None, None),
        P("col"),
    )
    out_specs = P("row", "col", None)
    return jax.shard_map(
        on_device, mesh=mesh, in_specs=in_specs, out_specs=out_specs, check_vma=False
    )
```

profile of v0, /device:TPU:0, one launch (start us, length us, event | category | flops | bytes accessed | tf_op | source)
XLA Modules:
  0.0 93.5 jit_solution(4920264722464064641)
XLA Ops:
  0.0 0.8 fusion.89
  0.8 4.9 %collective-permute-start = (bf16[1,48,256]{2,1,0:T(8,128)(2,1)S(1)}, bf16[1,48,256]{2,1,0:T(8,128)(2,1)S(1)}, u32[]{:S(2)}, u32[]{:S(2)}) collective-permute-start(bf16[1,48,256]{2,1,0:T(8,128)(2,1)S(1)} %get-tuple-element.22), channel_id=1, source_target_pairs={{0,16},{1,17},{2,18},{3,19},{4,20},{5,21},{6,22},{7,23},{8,24},{9,... | collective-permute-start | bytes 73736 | tf_op jit(solution)/shard_map/ppermute | solution.py:12
  5.6 1.3 %collective-permute-start.1 = (bf16[1,48,256]{2,1,0:T(8,128)(2,1)S(1)}, bf16[1,48,256]{2,1,0:T(8,128)(2,1)S(1)}, u32[]{:S(2)}, u32[]{:S(2)}) collective-permute-start(bf16[1,48,256]{2,1,0:T(8,128)(2,1)S(1)} %get-tuple-element.21), channel_id=1, source_target_pairs={{16,0},{17,1},{18,2},{19,3},{20,4},{21,5},{22,6},{23,7},{24,8},{25... | collective-permute-start | bytes 73736 | tf_op jit(solution)/shard_map/ppermute | solution.py:15
  7.1 4.2 %collective-permute-done.1 = bf16[1,48,256]{2,1,0:T(8,128)(2,1)S(1)} collective-permute-done((bf16[1,48,256]{2,1,0:T(8,128)(2,1)S(1)}, bf16[1,48,256]{2,1,0:T(8,128)(2,1)S(1)}, u32[]{:S(2)}, u32[]{:S(2)}) %collective-permute-start.1) | collective-permute-done | bytes 24608 | tf_op jit(solution)/shard_map/ppermute | solution.py:15
  11.3 2.2 %pad_maximum_fusion.4 = (bf16[32,48,256]{2,1,0:T(8,128)(2,1)S(1)}, bf16[32,48,256]{2,1,0:T(8,128)(2,1)S(1)}, bf16[34,48,256]{2,1,0:T(8,128)(2,1)S(1)}) fusion(bf16[32,48,256]{2,1,0:T(8,128)(2,1)} %param.7, bf16[1,48,256]{2,1,0:T(8,128)(2,1)S(1)} %collective-permute-done, bf16[1,48,256]{2,1,0:T(8,128)(2,1)S(1)} %collective-permute-done.1, ...), kind=kLoop, calls=%fused_computation.49 | loop fusion | flops 3145728 | bytes 3194880 | tf_op jit(solution)/shard_map/concatenate | solution.py:16
  13.6 1.3 %collective-permute-start.2 = (bf16[34,1,256]{2,1,0:T(2,128)(2,1)S(1)}, bf16[34,1,256]{2,1,0:T(2,128)(2,1)S(1)}, u32[]{:S(2)}, u32[]{:S(2)}) collective-permute-start(bf16[34,1,256]{2,1,0:T(2,128)(2,1)S(1)} %get-tuple-element.16), channel_id=1, source_target_pairs={{0,1},{1,2},{2,3},{3,4},{4,5},{5,6},{6,7},{7,8},{8,9},{9,10},{10,1... | collective-permute-start | bytes 52232 | tf_op jit(solution)/shard_map/ppermute | solution.py:12
  14.9 1.3 %collective-permute-start.3 = (bf16[34,1,256]{2,1,0:T(2,128)(2,1)S(1)}, bf16[34,1,256]{2,1,0:T(2,128)(2,1)S(1)}, u32[]{:S(2)}, u32[]{:S(2)}) collective-permute-start(bf16[34,1,256]{2,1,0:T(2,128)(2,1)S(1)} %get-tuple-element.17), channel_id=1, source_target_pairs={{1,0},{2,1},{3,2},{4,3},{5,4},{6,5},{7,6},{8,7},{9,8},{10,9},{11,1... | collective-permute-start | bytes 52232 | tf_op jit(solution)/shard_map/ppermute | solution.py:15
  17.0 2.8 %collective-permute-done.3 = bf16[34,1,256]{2,1,0:T(2,128)(2,1)S(1)} collective-permute-done((bf16[34,1,256]{2,1,0:T(2,128)(2,1)S(1)}, bf16[34,1,256]{2,1,0:T(2,128)(2,1)S(1)}, u32[]{:S(2)}, u32[]{:S(2)}) %collective-permute-start.3) | collective-permute-done | bytes 17440 | tf_op jit(solution)/shard_map/ppermute | solution.py:15
  19.8 2.9 %pad_maximum_fusion.3 = (bf16[32,48,256]{2,1,0:T(8,128)(2,1)S(1)}, bf16[32,48,256]{2,1,0:T(8,128)(2,1)S(1)}, bf16[32,48,256]{2,1,0:T(8,128)(2,1)S(1)}, bf16[32,4...) fusion(bf16[34,48,256]{2,1,0:T(8,128)(2,1)S(1)} %constant_dynamic-update-slice_fusion,, ...), kind=kLoop, calls=%fused_computation.48 | loop fusion | flops 9437184 | bytes 5588992 | tf_op jit(solution)/shard_map/concatenate | solution.py:16
  24.2 0.7 copy-done
  26.6 1.6 %collective-permute-start.4 = (bf16[1,48,256]{2,1,0:T(8,128)(2,1)S(1)}, bf16[1,48,256]{2,1,0:T(8,128)(2,1)S(1)}, u32[]{:S(2)}, u32[]{:S(2)}) collective-permute-start(bf16[1,48,256]{2,1,0:T(8,128)(2,1)S(1)} %slice.272), channel_id=1, source_target_pairs={{0,16},{1,17},{2,18},{3,19},{4,20},{5,21},{6,22},{7,23},{8,24},{9,... | collective-permute-start | bytes 73736 | tf_op jit(solution)/shard_map/ppermute | solution.py:23
  29.3 0.9 slice.237
  30.1 0.9 slice.239
  31.1 4.3 %collective-permute-start.5 = (bf16[33,1,256]{2,1,0:T(2,128)(2,1)S(1)}, bf16[33,1,256]{2,1,0:T(2,128)(2,1)S(1)}, u32[]{:S(2)}, u32[]{:S(2)}) collective-permute-start(bf16[33,1,256]{2,1,0:T(2,128)(2,1)S(1)} %fusion.66), channel_id=1, source_target_pairs={{0,1},{1,2},{2,3},{3,4},{4,5},{5,6},{6,7},{7,8},{8,9},{9,10},{10,1... | collective-permute-start | bytes 50696 | tf_op jit(solution)/shard_map/ppermute | solution.py:23
  36.0 1.2 %fusion.33 = f32[384,512]{1,0:T(8,128)S(1)} fusion(bf16[384,256]{1,0:T(8,128)(2,1)S(1)} %bitcast.192, bf16[3,3,256,512]{3,2,1,0:T(8,128)(2,1)} %param.10), kind=kOutput, calls=%fused_computation.76 | convolution fusion | flops 100663296 | bytes 1245184 | tf_op jit(solution)/shard_map/dot_general | solution.py:40
  37.2 5.0 %slice.227 = bf16[16,24,256]{2,1,0:T(8,128)(2,1)} slice(bf16[33,48,256]{2,1,0:T(8,128)(2,1)S(1)} %pad_maximum_fusion), slice={[0:31:2], [1:48:2], [0:256:1]} | slice | bytes 393216 | tf_op jit(solution)/shard_map/slice | solution.py:30
  42.2 0.5 maximum_maximum_fusion
  43.2 0.5 slice.229
  43.7 0.7 slice.235
  44.5 1.4 %convolution_add_fusion.20 = f32[384,512]{1,0:T(8,128)S(1)} fusion(f32[384,512]{1,0:T(8,128)S(1)} %fusion.33, bf16[384,256]{1,0:T(8,128)(2,1)S(1)} %bitcast.200, bf16[3,3,256,512]{3,2,1,0:T(8,128)(2,1)} %param.10), kind=kOutput, calls=%fused_computation.32 | convolution fusion | flops 100859904 | bytes 2031616 | tf_op jit(solution)/shard_map/dot_general | solution.py:40
  45.9 1.2 %convolution_add_fusion.19 = f32[384,512]{1,0:T(8,128)S(1)} fusion(f32[384,512]{1,0:T(8,128)S(1)} %convolution_add_fusion.20, bf16[384,256]{1,0:T(8,128)(2,1)S(1)} %bitcast.197, bf16[3,3,256,512]{3,2,1,0:T(8,128)(2,1)} %param.10), kind=kOutput, calls=%fused_computation.31 | convolution fusion | flops 100859904 | bytes 2031616 | tf_op jit(solution)/shard_map/dot_general | solution.py:40
  48.9 2.0 %copy.53 = bf16[16,24,512]{1,0,2:T(8,128)(2,1)S(1)} copy(bf16[16,24,512]{2,1,0:T(8,128)(2,1)S(1)} %maximum_convert_fusion.1) | data formatting | bytes 786432 | tf_op jit(solution)/shard_map/convert_element_type | solution.py:60
  50.9 2.7 %reshape.188 = bf16[16,2,6144]{2,1,0:T(2,128)(2,1)S(1)} reshape(bf16[512,16,24]{2,1,0:T(8,128)(2,1)S(1)} %bitcast.179) | data formatting | bytes 786432
  53.6 17.8 %all_to_all.18 = bf16[16,2,6144]{2,1,0:T(2,128)(2,1)S(1)} all-to-all(bf16[16,2,6144]{2,1,0:T(2,128)(2,1)S(1)} %reshape.188), channel_id=1, replica_groups=mesh['row'=2,'col'=16] {'col'}, dimensions={0} | all-to-all | bytes 786432 | tf_op jit(solution)/shard_map/all_to_all | solution.py:61
  71.5 3.0 %reshape.189 = bf16[512,16,24]{2,1,0:T(8,128)(2,1)S(1)} reshape(bf16[16,2,6144]{2,1,0:T(2,128)(2,1)S(1)} %all_to_all.18) | data formatting | bytes 786432
  74.4 3.1 %copy.67 = bf16[16,24,16,32]{3,2,1,0:T(8,128)(2,1)} copy(bf16[16,24,16,32]{1,0,3,2:T(8,128)(2,1)S(1)} %bitcast.177) | data formatting | bytes 786432 | tf_op jit(solution)/shard_map/all_to_all | solution.py:61
  77.5 1.0 %fusion.87 = (bf16[1,16,24,32]{3,1,2,0:T(8,128)(2,1)S(1)}, bf16[1,16,24,32]{3,1,2,0:T(8,128)(2,1)S(1)}) fusion(bf16[16,16,24,32]{3,1,2,0:T(8,128)(2,1)} %bitcast.191), kind=kLoop, calls=%fused_computation.133 | loop fusion | bytes 98304 | tf_op jit(solution)/shard_map/slice | solution.py:13
  78.8 2.8 %collective-permute-start.6 = (bf16[1,384,32]{1,2,0:T(8,128)(2,1)S(1)}, bf16[1,384,32]{1,2,0:T(8,128)(2,1)S(1)}, u32[]{:S(2)}, u32[]{:S(2)}) collective-permute-start(bf16[1,384,32]{1,2,0:T(8,128)(2,1)S(1)} %slice.242), channel_id=1, source_target_pairs={{0,16},{1,17},{2,18},{3,19},{4,20},{5,21},{6,22},{7,23},{8,24},{9,... | collective-permute-start | bytes 73736 | tf_op jit(solution)/shard_map/ppermute | solution.py:12
  82.0 1.5 %collective-permute-start.7 = (bf16[1,384,32]{1,2,0:T(8,128)(2,1)S(1)}, bf16[1,384,32]{1,2,0:T(8,128)(2,1)S(1)}, u32[]{:S(2)}, u32[]{:S(2)}) collective-permute-start(bf16[1,384,32]{1,2,0:T(8,128)(2,1)S(1)} %slice.244), channel_id=1, source_target_pairs={{16,0},{17,1},{18,2},{19,3},{20,4},{21,5},{22,6},{23,7},{24,8},{25... | collective-permute-start | bytes 73736 | tf_op jit(solution)/shard_map/ppermute | solution.py:15
  83.5 2.7 %copy.56 = bf16[16,16,24,32]{2,1,3,0:T(8,128)(2,1)} copy(bf16[16,16,24,32]{2,0,3,1:T(8,128)(2,1)S(1)} %bitcast.178) | data formatting | bytes 786432 | tf_op jit(solution)/shard_map/all_to_all | solution.py:61
  86.2 3.4 %all_to_all.16 = bf16[16,384,32]{1,2,0:T(8,128)(2,1)S(1)} reshape(bf16[16,16,24,32]{2,1,3,0:T(8,128)(2,1)} %copy.56) | data formatting | bytes 786432 | tf_op jit(solution)/shard_map/all_to_all | solution.py:61
  92.5 1.0 %fusion.5 = bf16[16,32,384]{2,1,0:T(8,128)(2,1)} fusion(f32[16,384,32]{1,2,0:T(8,128)S(1)} %fusion.16, f32[16,384,32]{1,2,0:T(8,128)S(1)} %convolution_add_fusion.7, bf16[1,384,32]{1,2,0:T(8,128)(2,1)S(1)} %collective-permute-done.7, bf16[16,384,32]{1,2,0:T(8,128)(2,1)S(1)} %all_to_all.16, f32[32]{0:T(128)S(1)} %copy-done.7, ...), kind=kOutput, calls=%fused_computation.33 | convolution fusion | flops 14155776 | bytes 2392576 | tf_op jit(solution)/shard_map/rwgi,gio->rgow/dot_general | solution.py:74
  (61 shorter events, 11.5 us)
Async XLA Ops:
  0.8 6.4 %collective-permute-start = (bf16[1,48,256]{2,1,0:T(8,128)(2,1)S(1)}, bf16[1,48,256]{2,1,0:T(8,128)(2,1)S(1)}, u32[]{:S(2)}, u32[]{:S(2)}) collective-permute-start(bf16[1,48,256]{2,1,0:T(8,128)(2,1)S(1)} %get-tuple-element.22), channel_id=1, source_target_pairs={{0,16},{1,17},{2,18},{3,19},{4,20},{5,21},{6,22},{7,23},{8,24},{9,... | collective-permute-start | bytes 73736 | tf_op jit(solution)/shard_map/ppermute | solution.py:12
  5.6 5.7 %collective-permute-start.1 = (bf16[1,48,256]{2,1,0:T(8,128)(2,1)S(1)}, bf16[1,48,256]{2,1,0:T(8,128)(2,1)S(1)}, u32[]{:S(2)}, u32[]{:S(2)}) collective-permute-start(bf16[1,48,256]{2,1,0:T(8,128)(2,1)S(1)} %get-tuple-element.21), channel_id=1, source_target_pairs={{16,0},{17,1},{18,2},{19,3},{20,4},{21,5},{22,6},{23,7},{24,8},{25... | collective-permute-start | bytes 73736 | tf_op jit(solution)/shard_map/ppermute | solution.py:15
  7.1 9.1 %copy-start.2 = (bf16[3,3,256,256]{3,2,1,0:T(8,128)(2,1)S(1)}, bf16[3,3,256,256]{3,2,1,0:T(8,128)(2,1)}, u32[]{:S(2)}) copy-start(bf16[3,3,256,256]{3,2,1,0:T(8,128)(2,1)} %param.8) | copy-start | bytes 3538948
  13.6 3.3 %collective-permute-start.2 = (bf16[34,1,256]{2,1,0:T(2,128)(2,1)S(1)}, bf16[34,1,256]{2,1,0:T(2,128)(2,1)S(1)}, u32[]{:S(2)}, u32[]{:S(2)}) collective-permute-start(bf16[34,1,256]{2,1,0:T(2,128)(2,1)S(1)} %get-tuple-element.16), channel_id=1, source_target_pairs={{0,1},{1,2},{2,3},{3,4},{4,5},{5,6},{6,7},{7,8},{8,9},{9,10},{10,1... | collective-permute-start | bytes 52232 | tf_op jit(solution)/shard_map/ppermute | solution.py:12
  14.9 4.9 %collective-permute-start.3 = (bf16[34,1,256]{2,1,0:T(2,128)(2,1)S(1)}, bf16[34,1,256]{2,1,0:T(2,128)(2,1)S(1)}, u32[]{:S(2)}, u32[]{:S(2)}) collective-permute-start(bf16[34,1,256]{2,1,0:T(2,128)(2,1)S(1)} %get-tuple-element.17), channel_id=1, source_target_pairs={{1,0},{2,1},{3,2},{4,3},{5,4},{6,5},{7,6},{8,7},{9,8},{10,9},{11,1... | collective-permute-start | bytes 52232 | tf_op jit(solution)/shard_map/ppermute | solution.py:15
  23.8 1.1 %copy-start = (bf16[32,48,256]{2,1,0:T(8,128)(2,1)S(1)}, bf16[32,48,256]{2,1,0:T(8,128)(2,1)}, u32[]{:S(2)}) copy-start(bf16[32,48,256]{2,1,0:T(8,128)(2,1)} %param.7) | copy-start | bytes 2359300
  25.7 0.7 copy-start.6
  26.6 4.4 %collective-permute-start.4 = (bf16[1,48,256]{2,1,0:T(8,128)(2,1)S(1)}, bf16[1,48,256]{2,1,0:T(8,128)(2,1)S(1)}, u32[]{:S(2)}, u32[]{:S(2)}) collective-permute-start(bf16[1,48,256]{2,1,0:T(8,128)(2,1)S(1)} %slice.272), channel_id=1, source_target_pairs={{0,16},{1,17},{2,18},{3,19},{4,20},{5,21},{6,22},{7,23},{8,24},{9,... | collective-permute-start | bytes 73736 | tf_op jit(solution)/shard_map/ppermute | solution.py:23
  31.1 11.1 %collective-permute-start.5 = (bf16[33,1,256]{2,1,0:T(2,128)(2,1)S(1)}, bf16[33,1,256]{2,1,0:T(2,128)(2,1)S(1)}, u32[]{:S(2)}, u32[]{:S(2)}) collective-permute-start(bf16[33,1,256]{2,1,0:T(2,128)(2,1)S(1)} %fusion.66), channel_id=1, source_target_pairs={{0,1},{1,2},{2,3},{3,4},{4,5},{5,6},{6,7},{7,8},{8,9},{9,10},{10,1... | collective-permute-start | bytes 50696 | tf_op jit(solution)/shard_map/ppermute | solution.py:23
  42.7 3.2 %copy-start.3 = (bf16[16,24,256]{2,1,0:T(8,128)(2,1)S(1)}, bf16[16,24,256]{2,1,0:T(8,128)(2,1)}, u32[]{:S(2)}) copy-start(bf16[16,24,256]{2,1,0:T(8,128)(2,1)} %slice.227) | copy-start | bytes 589828
  44.5 2.6 %copy-start.1 = (bf16[3,3,256,512]{3,2,1,0:T(8,128)(2,1)S(1)}, bf16[3,3,256,512]{3,2,1,0:T(8,128)(2,1)}, u32[]{:S(2)}) copy-start(bf16[3,3,256,512]{3,2,1,0:T(8,128)(2,1)} %param.10) | copy-start | bytes 7077892
  48.2 0.7 copy-start.5
  78.8 10.8 %collective-permute-start.6 = (bf16[1,384,32]{1,2,0:T(8,128)(2,1)S(1)}, bf16[1,384,32]{1,2,0:T(8,128)(2,1)S(1)}, u32[]{:S(2)}, u32[]{:S(2)}) collective-permute-start(bf16[1,384,32]{1,2,0:T(8,128)(2,1)S(1)} %slice.242), channel_id=1, source_target_pairs={{0,16},{1,17},{2,18},{3,19},{4,20},{5,21},{6,22},{7,23},{8,24},{9,... | collective-permute-start | bytes 73736 | tf_op jit(solution)/shard_map/ppermute | solution.py:12
  82.0 7.6 %collective-permute-start.7 = (bf16[1,384,32]{1,2,0:T(8,128)(2,1)S(1)}, bf16[1,384,32]{1,2,0:T(8,128)(2,1)S(1)}, u32[]{:S(2)}, u32[]{:S(2)}) collective-permute-start(bf16[1,384,32]{1,2,0:T(8,128)(2,1)S(1)} %slice.244), channel_id=1, source_target_pairs={{16,0},{17,1},{18,2},{19,3},{20,4},{21,5},{22,6},{23,7},{24,8},{25... | collective-permute-start | bytes 73736 | tf_op jit(solution)/shard_map/ppermute | solution.py:15
  86.2 3.8 %copy-start.4 = (bf16[1,3,3,32,32]{4,3,2,1,0:T(8,128)(2,1)S(1)}, bf16[1,3,3,32,32]{4,3,2,1,0:T(8,128)(2,1)}, u32[]{:S(2)}) copy-start(bf16[1,3,3,32,32]{4,3,2,1,0:T(8,128)(2,1)} %param.12) | copy-start | bytes 55300
  91.8 0.7 copy-start.7
where the time goes:
time: 94.2 us; the launch traced here: 93.5 us
  local copies, waits for them, and re-layouts  30.4 us (32%)
  starting transfers between devices  18.9 us (20%)
  blocking collectives  17.8 us (19%)
  matrix products  12.2 us (13%)
  waiting for transfers between devices  7.24 us (8%)
  other arithmetic  6.36 us (7%)
    all_to_all x1, blocking collectives, on_device(): lax.all_to_all(layer_two, 'col', split_axis=2, concat_axis=1, tiled=True)  17.8 us
    slice x9, local copies, waits for them, and re-layouts, conv_taps(): lax.slice(padded, (tap_row, tap_col, 0), (tap_row + stride * (out_rows -...  9.99 us
    all_to_all x3, local copies, waits for them, and re-layouts, on_device(): lax.all_to_all(layer_two, 'col', split_axis=2, concat_axis=1, tiled=True)  9.22 us
    ppermute x3, starting transfers between devices, padded_2(): lax.ppermute(lax.slice_in_dim(block, block.shape[dim] - width, None, axis...  8.97 us
    dot_general x18, matrix products, conv_taps(): jnp.dot(window.reshape(out_rows * out_cols, padded.shape[2]), weight[tap_...  8.73 us
    ppermute x3, waiting for transfers between devices, padded_2(): lax.ppermute(lax.slice_in_dim(block, 0, width, axis=dim), axis, backward)  7.03 us
    unnamed x19, local copies, waits for them, and re-layouts  6.77 us
    ppermute x2, starting transfers between devices, passed_along(): return lax.ppermute(block, axis, route)  5.91 us
  transfers between devices with their start and end apart: 8, of which 3 were waited for; matrix products, arithmetic and copies ran while one was open for 14% of the time, Pallas kernels for 0%

commit v1 on v0

--- a/solution.py
+++ b/solution.py
@@ -58,7 +58,10 @@
     extended = jnp.concatenate([left_column, extended], 1)
     summed = conv_taps(extended, conv_two, tile_rows // 2, tile_cols // 2, 2)
     layer_two = jax.nn.relu(summed + bias_two).astype(jnp.bfloat16)
-    grouped = lax.all_to_all(layer_two, "col", split_axis=2, concat_axis=1, tiled=True)
+    grouped = jnp.concatenate(
+        lax.all_to_all(jnp.stack(jnp.split(layer_two, lax.axis_size("col"), axis=2)), "col", 0, 0),
+        axis=1,
+    )
     grouped = padded_2(grouped, (("row", 0),), 1)
     grouped = jnp.pad(grouped, ((0, 0), (1, 1), (0, 0)))
     local_groups = conv_three.shape[0]

time: 94.2 us -> 85.5 us (0.908)
  local copies, waits for them, and re-layouts: 30.4 us -> 21.7 us
    all_to_all x3 -> x0, local copies, waits for them, and re-layouts: 9.22 us -> none  [on_device(): lax.all_to_all(layer_two, 'col', split_axis=2, concat_axis=1, tiled=True)]
    reshape x0 -> x2, local copies, waits for them, and re-layouts: none -> 5.87 us  [on_device(): jnp.concatenate(lax.all_to_all(jnp.stack(jnp.split(layer_two, lax.axis_si...]
    unnamed x19 -> x36, local copies, waits for them, and re-layouts: 6.77 us -> 4.67 us
    convert_element_type x1 -> x0, local copies, waits for them, and re-layouts: 1.97 us -> none  [on_device(): layer_two = jax.nn.relu(summed + bias_two).astype(jnp.bfloat16)]
    slice x4 -> x3, local copies, waits for them, and re-layouts: 1.37 us -> 0.17 us  [padded_2(): lax.slice_in_dim(block, block.shape[dim] - width, None, axis=dim)]
  transfers between devices with their start and end apart: 8 -> 8, of which waited for: 3 -> 3; matrix products, arithmetic and copies ran while one was open for 14% -> 19% of each run, Pallas kernels for 0% -> 0%
where the time goes in v1:
time: 85.5 us; the launch traced here: 84.9 us
  local copies, waits for them, and re-layouts  21.7 us (25%)
  starting transfers between devices  18.9 us (22%)
  blocking collectives  17.8 us (21%)
  matrix products  12.2 us (14%)
  waiting for transfers between devices  7.24 us (8%)
  other arithmetic  6.36 us (7%)
    all_to_all x1, blocking collectives, on_device(): lax.all_to_all(jnp.stack(jnp.split(layer_two, lax.axis_size('col'), axis=...  17.8 us
    slice x9, local copies, waits for them, and re-layouts, conv_taps(): lax.slice(padded, (tap_row, tap_col, 0), (tap_row + stride * (out_rows -...  9.99 us
    ppermute x3, starting transfers between devices, padded_2(): lax.ppermute(lax.slice_in_dim(block, block.shape[dim] - width, None, axis...  8.98 us
    dot_general x18, matrix products, conv_taps(): jnp.dot(window.reshape(out_rows * out_cols, padded.shape[2]), weight[tap_...  8.73 us
    ppermute x3, waiting for transfers between devices, padded_2(): lax.ppermute(lax.slice_in_dim(block, 0, width, axis=dim), axis, backward)  7.03 us
    ppermute x2, starting transfers between devices, passed_along(): return lax.ppermute(block, axis, route)  5.91 us
    reshape x2, local copies, waits for them, and re-layouts, on_device(): jnp.concatenate(lax.all_to_all(jnp.stack(jnp.split(layer_two, lax.axis_si...  5.87 us
    concatenate x3, other arithmetic, padded_2(): block = jnp.concatenate([low, block, high], axis=dim)  5.43 us
  transfers between devices with their start and end apart: 8, of which 3 were waited for; matrix products, arithmetic and copies ran while one was open for 19% of the time, Pallas kernels for 0%

profile of v1, /device:TPU:0, one launch (start us, length us, event | category | flops | bytes accessed | tf_op | source)
XLA Modules:
  0.0 84.9 jit_solution(3738763883437311325)
XLA Ops:
  0.0 0.8 fusion.105
  0.8 4.9 %collective-permute-start = (bf16[1,48,256]{2,1,0:T(8,128)(2,1)S(1)}, bf16[1,48,256]{2,1,0:T(8,128)(2,1)S(1)}, u32[]{:S(2)}, u32[]{:S(2)}) collective-permute-start(bf16[1,48,256]{2,1,0:T(8,128)(2,1)S(1)} %get-tuple-element.22), channel_id=1, source_target_pairs={{0,16},{1,17},{2,18},{3,19},{4,20},{5,21},{6,22},{7,23},{8,24},{9,... | collective-permute-start | bytes 73736 | tf_op jit(solution)/shard_map/ppermute | solution.py:12
  5.6 1.3 %collective-permute-start.1 = (bf16[1,48,256]{2,1,0:T(8,128)(2,1)S(1)}, bf16[1,48,256]{2,1,0:T(8,128)(2,1)S(1)}, u32[]{:S(2)}, u32[]{:S(2)}) collective-permute-start(bf16[1,48,256]{2,1,0:T(8,128)(2,1)S(1)} %get-tuple-element.21), channel_id=1, source_target_pairs={{16,0},{17,1},{18,2},{19,3},{20,4},{21,5},{22,6},{23,7},{24,8},{25... | collective-permute-start | bytes 73736 | tf_op jit(solution)/shard_map/ppermute | solution.py:15
  7.1 4.2 %collective-permute-done.1 = bf16[1,48,256]{2,1,0:T(8,128)(2,1)S(1)} collective-permute-done((bf16[1,48,256]{2,1,0:T(8,128)(2,1)S(1)}, bf16[1,48,256]{2,1,0:T(8,128)(2,1)S(1)}, u32[]{:S(2)}, u32[]{:S(2)}) %collective-permute-start.1) | collective-permute-done | bytes 24608 | tf_op jit(solution)/shard_map/ppermute | solution.py:15
  11.3 2.2 %pad_maximum_fusion.4 = (bf16[32,48,256]{2,1,0:T(8,128)(2,1)S(1)}, bf16[32,48,256]{2,1,0:T(8,128)(2,1)S(1)}, bf16[34,48,256]{2,1,0:T(8,128)(2,1)S(1)}) fusion(bf16[32,48,256]{2,1,0:T(8,128)(2,1)} %param.7, bf16[1,48,256]{2,1,0:T(8,128)(2,1)S(1)} %collective-permute-done, bf16[1,48,256]{2,1,0:T(8,128)(2,1)S(1)} %collective-permute-done.1, ...), kind=kLoop, calls=%fused_computation.49 | loop fusion | flops 3145728 | bytes 3194880 | tf_op jit(solution)/shard_map/concatenate | solution.py:16
  13.6 1.3 %collective-permute-start.2 = (bf16[34,1,256]{2,1,0:T(2,128)(2,1)S(1)}, bf16[34,1,256]{2,1,0:T(2,128)(2,1)S(1)}, u32[]{:S(2)}, u32[]{:S(2)}) collective-permute-start(bf16[34,1,256]{2,1,0:T(2,128)(2,1)S(1)} %get-tuple-element.16), channel_id=1, source_target_pairs={{0,1},{1,2},{2,3},{3,4},{4,5},{5,6},{6,7},{7,8},{8,9},{9,10},{10,1... | collective-permute-start | bytes 52232 | tf_op jit(solution)/shard_map/ppermute | solution.py:12
  14.9 1.3 %collective-permute-start.3 = (bf16[34,1,256]{2,1,0:T(2,128)(2,1)S(1)}, bf16[34,1,256]{2,1,0:T(2,128)(2,1)S(1)}, u32[]{:S(2)}, u32[]{:S(2)}) collective-permute-start(bf16[34,1,256]{2,1,0:T(2,128)(2,1)S(1)} %get-tuple-element.17), channel_id=1, source_target_pairs={{1,0},{2,1},{3,2},{4,3},{5,4},{6,5},{7,6},{8,7},{9,8},{10,9},{11,1... | collective-permute-start | bytes 52232 | tf_op jit(solution)/shard_map/ppermute | solution.py:15
  17.0 2.8 %collective-permute-done.3 = bf16[34,1,256]{2,1,0:T(2,128)(2,1)S(1)} collective-permute-done((bf16[34,1,256]{2,1,0:T(2,128)(2,1)S(1)}, bf16[34,1,256]{2,1,0:T(2,128)(2,1)S(1)}, u32[]{:S(2)}, u32[]{:S(2)}) %collective-permute-start.3) | collective-permute-done | bytes 17440 | tf_op jit(solution)/shard_map/ppermute | solution.py:15
  19.8 2.9 %pad_maximum_fusion.3 = (bf16[32,48,256]{2,1,0:T(8,128)(2,1)S(1)}, bf16[32,48,256]{2,1,0:T(8,128)(2,1)S(1)}, bf16[32,48,256]{2,1,0:T(8,128)(2,1)S(1)}, bf16[32,4...) fusion(bf16[34,48,256]{2,1,0:T(8,128)(2,1)S(1)} %constant_dynamic-update-slice_fusion,, ...), kind=kLoop, calls=%fused_computation.48 | loop fusion | flops 9437184 | bytes 5588992 | tf_op jit(solution)/shard_map/concatenate | solution.py:16
  24.2 0.7 copy-done.1
  26.6 1.6 %collective-permute-start.4 = (bf16[1,48,256]{2,1,0:T(8,128)(2,1)S(1)}, bf16[1,48,256]{2,1,0:T(8,128)(2,1)S(1)}, u32[]{:S(2)}, u32[]{:S(2)}) collective-permute-start(bf16[1,48,256]{2,1,0:T(8,128)(2,1)S(1)} %slice.272), channel_id=1, source_target_pairs={{0,16},{1,17},{2,18},{3,19},{4,20},{5,21},{6,22},{7,23},{8,24},{9,... | collective-permute-start | bytes 73736 | tf_op jit(solution)/shard_map/ppermute | solution.py:23
  28.2 0.5 slice.231
  28.8 0.5 slice.233
  29.3 0.9 %slice.237 = bf16[16,24,256]{2,1,0:T(8,128)(2,1)S(1)} slice(bf16[32,48,256]{2,1,0:T(8,128)(2,1)S(1)} %maximum_convert_fusion), slice={[1:32:2], [0:47:2], [0:256:1]} | slice | bytes 393216 | tf_op jit(solution)/shard_map/slice | solution.py:30
  30.1 0.9 %slice.239 = bf16[16,24,256]{2,1,0:T(8,128)(2,1)S(1)} slice(bf16[32,48,256]{2,1,0:T(8,128)(2,1)S(1)} %maximum_convert_fusion), slice={[1:32:2], [1:48:2], [0:256:1]} | slice | bytes 393216 | tf_op jit(solution)/shard_map/slice | solution.py:30
  31.1 4.3 %collective-permute-start.5 = (bf16[33,1,256]{2,1,0:T(2,128)(2,1)S(1)}, bf16[33,1,256]{2,1,0:T(2,128)(2,1)S(1)}, u32[]{:S(2)}, u32[]{:S(2)}) collective-permute-start(bf16[33,1,256]{2,1,0:T(2,128)(2,1)S(1)} %fusion.82), channel_id=1, source_target_pairs={{0,1},{1,2},{2,3},{3,4},{4,5},{5,6},{6,7},{7,8},{8,9},{9,10},{10,1... | collective-permute-start | bytes 50696 | tf_op jit(solution)/shard_map/ppermute | solution.py:23
  36.0 1.2 %fusion.33 = f32[384,512]{1,0:T(8,128)S(1)} fusion(bf16[384,256]{1,0:T(8,128)(2,1)S(1)} %bitcast.243, bf16[3,3,256,512]{3,2,1,0:T(8,128)(2,1)} %param.10), kind=kOutput, calls=%fused_computation.76 | convolution fusion | flops 100663296 | bytes 1245184 | tf_op jit(solution)/shard_map/dot_general | solution.py:40
  37.2 5.0 %slice.227 = bf16[16,24,256]{2,1,0:T(8,128)(2,1)} slice(bf16[33,48,256]{2,1,0:T(8,128)(2,1)S(1)} %pad_maximum_fusion), slice={[0:31:2], [1:48:2], [0:256:1]} | slice | bytes 393216 | tf_op jit(solution)/shard_map/slice | solution.py:30
  42.2 0.5 maximum_maximum_fusion
  42.7 0.5 slice.223
  43.2 0.5 slice.229
  43.7 0.7 slice.235
  44.5 1.4 %convolution_add_fusion.20 = f32[384,512]{1,0:T(8,128)S(1)} fusion(f32[384,512]{1,0:T(8,128)S(1)} %fusion.33, bf16[384,256]{1,0:T(8,128)(2,1)S(1)} %bitcast.251, bf16[3,3,256,512]{3,2,1,0:T(8,128)(2,1)} %param.10), kind=kOutput, calls=%fused_computation.32 | convolution fusion | flops 100859904 | bytes 2031616 | tf_op jit(solution)/shard_map/dot_general | solution.py:40
  45.9 1.2 %convolution_add_fusion.19 = f32[384,512]{1,0:T(8,128)S(1)} fusion(f32[384,512]{1,0:T(8,128)S(1)} %convolution_add_fusion.20, bf16[384,256]{1,0:T(8,128)(2,1)S(1)} %bitcast.248, bf16[3,3,256,512]{3,2,1,0:T(8,128)(2,1)} %param.10), kind=kOutput, calls=%fused_computation.31 | convolution fusion | flops 100859904 | bytes 2031616 | tf_op jit(solution)/shard_map/dot_general | solution.py:40
  50.5 1.5 %reshape.196 = bf16[16,2,6144]{2,1,0:T(2,128)(2,1)S(1)} reshape(bf16[16,16,24,32]{3,2,1,0:T(8,128)(2,1)S(1)} %fusion.66) | data formatting | bytes 786432
  52.0 17.8 %all_to_all.5 = bf16[16,2,6144]{2,1,0:T(2,128)(2,1)S(1)} all-to-all(bf16[16,2,6144]{2,1,0:T(2,128)(2,1)S(1)} %reshape.196), channel_id=1, replica_groups=mesh['row'=2,'col'=16] {'col'}, dimensions={0} | all-to-all | bytes 786432 | tf_op jit(solution)/shard_map/all_to_all | solution.py:62
  69.8 0.8 reshape.197
  70.7 2.8 %collective-permute-start.6 = (bf16[1,384,32]{1,2,0:T(8,128)(2,1)S(1)}, bf16[1,384,32]{1,2,0:T(8,128)(2,1)S(1)}, u32[]{:S(2)}, u32[]{:S(2)}) collective-permute-start(bf16[1,384,32]{1,2,0:T(8,128)(2,1)S(1)} %copy.57), channel_id=1, source_target_pairs={{0,16},{1,17},{2,18},{3,19},{4,20},{5,21},{6,22},{7,23},{8,24},{9,... | collective-permute-start | bytes 73736 | tf_op jit(solution)/shard_map/ppermute | solution.py:12
  73.6 1.5 %collective-permute-start.7 = (bf16[1,384,32]{1,2,0:T(8,128)(2,1)S(1)}, bf16[1,384,32]{1,2,0:T(8,128)(2,1)S(1)}, u32[]{:S(2)}, u32[]{:S(2)}) collective-permute-start(bf16[1,384,32]{1,2,0:T(8,128)(2,1)S(1)} %copy.58), channel_id=1, source_target_pairs={{16,0},{17,1},{18,2},{19,3},{20,4},{21,5},{22,6},{23,7},{24,8},{25... | collective-permute-start | bytes 73736 | tf_op jit(solution)/shard_map/ppermute | solution.py:15
  75.1 3.6 %copy.46 = bf16[16,16,24,32]{2,1,3,0:T(8,128)(2,1)S(1)} copy(bf16[16,16,24,32]{3,2,0,1:T(8,128)(2,1)} %bitcast.231) | data formatting | bytes 786432 | tf_op jit(solution)/shard_map/reshape | solution.py:61
  78.7 2.3 %reshape.171 = bf16[16,384,32]{1,2,0:T(8,128)(2,1)S(1)} reshape(bf16[16,16,24,32]{2,1,3,0:T(8,128)(2,1)S(1)} %copy.46) | data formatting | bytes 786432 | tf_op jit(solution)/shard_map/reshape | solution.py:61
  83.9 1.0 %fusion.5 = bf16[16,32,384]{2,1,0:T(8,128)(2,1)} fusion(f32[16,384,32]{1,2,0:T(8,128)S(1)} %fusion.16, f32[16,384,32]{1,2,0:T(8,128)S(1)} %convolution_add_fusion.7, bf16[1,384,32]{1,2,0:T(8,128)(2,1)S(1)} %collective-permute-done.7, bf16[16,384,32]{1,2,0:T(8,128)(2,1)S(1)} %reshape.171, f32[32]{0:T(128)S(1)} %copy-done.8, ...), kind=kOutput, calls=%fused_computation.33 | convolution fusion | flops 14155776 | bytes 2392576 | tf_op jit(solution)/shard_map/rwgi,gio->rgow/dot_general | solution.py:77
  (75 shorter events, 10.9 us)
Async XLA Ops:
  0.8 6.4 %collective-permute-start = (bf16[1,48,256]{2,1,0:T(8,128)(2,1)S(1)}, bf16[1,48,256]{2,1,0:T(8,128)(2,1)S(1)}, u32[]{:S(2)}, u32[]{:S(2)}) collective-permute-start(bf16[1,48,256]{2,1,0:T(8,128)(2,1)S(1)} %get-tuple-element.22), channel_id=1, source_target_pairs={{0,16},{1,17},{2,18},{3,19},{4,20},{5,21},{6,22},{7,23},{8,24},{9,... | collective-permute-start | bytes 73736 | tf_op jit(solution)/shard_map/ppermute | solution.py:12
  5.6 5.7 %collective-permute-start.1 = (bf16[1,48,256]{2,1,0:T(8,128)(2,1)S(1)}, bf16[1,48,256]{2,1,0:T(8,128)(2,1)S(1)}, u32[]{:S(2)}, u32[]{:S(2)}) collective-permute-start(bf16[1,48,256]{2,1,0:T(8,128)(2,1)S(1)} %get-tuple-element.21), channel_id=1, source_target_pairs={{16,0},{17,1},{18,2},{19,3},{20,4},{21,5},{22,6},{23,7},{24,8},{25... | collective-permute-start | bytes 73736 | tf_op jit(solution)/shard_map/ppermute | solution.py:15
  7.1 9.1 %copy-start.3 = (bf16[3,3,256,256]{3,2,1,0:T(8,128)(2,1)S(1)}, bf16[3,3,256,256]{3,2,1,0:T(8,128)(2,1)}, u32[]{:S(2)}) copy-start(bf16[3,3,256,256]{3,2,1,0:T(8,128)(2,1)} %param.8) | copy-start | bytes 3538948
  13.6 3.3 %collective-permute-start.2 = (bf16[34,1,256]{2,1,0:T(2,128)(2,1)S(1)}, bf16[34,1,256]{2,1,0:T(2,128)(2,1)S(1)}, u32[]{:S(2)}, u32[]{:S(2)}) collective-permute-start(bf16[34,1,256]{2,1,0:T(2,128)(2,1)S(1)} %get-tuple-element.16), channel_id=1, source_target_pairs={{0,1},{1,2},{2,3},{3,4},{4,5},{5,6},{6,7},{7,8},{8,9},{9,10},{10,1... | collective-permute-start | bytes 52232 | tf_op jit(solution)/shard_map/ppermute | solution.py:12
  14.9 4.9 %collective-permute-start.3 = (bf16[34,1,256]{2,1,0:T(2,128)(2,1)S(1)}, bf16[34,1,256]{2,1,0:T(2,128)(2,1)S(1)}, u32[]{:S(2)}, u32[]{:S(2)}) collective-permute-start(bf16[34,1,256]{2,1,0:T(2,128)(2,1)S(1)} %get-tuple-element.17), channel_id=1, source_target_pairs={{1,0},{2,1},{3,2},{4,3},{5,4},{6,5},{7,6},{8,7},{9,8},{10,9},{11,1... | collective-permute-start | bytes 52232 | tf_op jit(solution)/shard_map/ppermute | solution.py:15
  23.8 1.1 %copy-start.1 = (bf16[32,48,256]{2,1,0:T(8,128)(2,1)S(1)}, bf16[32,48,256]{2,1,0:T(8,128)(2,1)}, u32[]{:S(2)}) copy-start(bf16[32,48,256]{2,1,0:T(8,128)(2,1)} %param.7) | copy-start | bytes 2359300
  25.7 0.7 copy-start.7
  26.6 4.4 %collective-permute-start.4 = (bf16[1,48,256]{2,1,0:T(8,128)(2,1)S(1)}, bf16[1,48,256]{2,1,0:T(8,128)(2,1)S(1)}, u32[]{:S(2)}, u32[]{:S(2)}) collective-permute-start(bf16[1,48,256]{2,1,0:T(8,128)(2,1)S(1)} %slice.272), channel_id=1, source_target_pairs={{0,16},{1,17},{2,18},{3,19},{4,20},{5,21},{6,22},{7,23},{8,24},{9,... | collective-permute-start | bytes 73736 | tf_op jit(solution)/shard_map/ppermute | solution.py:23
  31.1 11.1 %collective-permute-start.5 = (bf16[33,1,256]{2,1,0:T(2,128)(2,1)S(1)}, bf16[33,1,256]{2,1,0:T(2,128)(2,1)S(1)}, u32[]{:S(2)}, u32[]{:S(2)}) collective-permute-start(bf16[33,1,256]{2,1,0:T(2,128)(2,1)S(1)} %fusion.82), channel_id=1, source_target_pairs={{0,1},{1,2},{2,3},{3,4},{4,5},{5,6},{6,7},{7,8},{8,9},{9,10},{10,1... | collective-permute-start | bytes 50696 | tf_op jit(solution)/shard_map/ppermute | solution.py:23
  42.7 3.2 %copy-start.4 = (bf16[16,24,256]{2,1,0:T(8,128)(2,1)S(1)}, bf16[16,24,256]{2,1,0:T(8,128)(2,1)}, u32[]{:S(2)}) copy-start(bf16[16,24,256]{2,1,0:T(8,128)(2,1)} %slice.227) | copy-start | bytes 589828
  44.5 2.6 %copy-start.2 = (bf16[3,3,256,512]{3,2,1,0:T(8,128)(2,1)S(1)}, bf16[3,3,256,512]{3,2,1,0:T(8,128)(2,1)}, u32[]{:S(2)}) copy-start(bf16[3,3,256,512]{3,2,1,0:T(8,128)(2,1)} %param.10) | copy-start | bytes 7077892
  48.2 0.7 copy-start.6
  70.6 3.1 %copy-start = (bf16[16,16,24,32]{3,2,1,0:T(8,128)(2,1)}, bf16[16,16,24,32]{3,2,1,0:T(8,128)(2,1)S(1)}, u32[]{:S(2)}) copy-start(bf16[16,16,24,32]{3,2,1,0:T(8,128)(2,1)S(1)} %reshape.197) | copy-start | bytes 1179652
  70.7 10.3 %collective-permute-start.6 = (bf16[1,384,32]{1,2,0:T(8,128)(2,1)S(1)}, bf16[1,384,32]{1,2,0:T(8,128)(2,1)S(1)}, u32[]{:S(2)}, u32[]{:S(2)}) collective-permute-start(bf16[1,384,32]{1,2,0:T(8,128)(2,1)S(1)} %copy.57), channel_id=1, source_target_pairs={{0,16},{1,17},{2,18},{3,19},{4,20},{5,21},{6,22},{7,23},{8,24},{9,... | collective-permute-start | bytes 73736 | tf_op jit(solution)/shard_map/ppermute | solution.py:12
  73.6 7.4 %collective-permute-start.7 = (bf16[1,384,32]{1,2,0:T(8,128)(2,1)S(1)}, bf16[1,384,32]{1,2,0:T(8,128)(2,1)S(1)}, u32[]{:S(2)}, u32[]{:S(2)}) collective-permute-start(bf16[1,384,32]{1,2,0:T(8,128)(2,1)S(1)} %copy.58), channel_id=1, source_target_pairs={{16,0},{17,1},{18,2},{19,3},{20,4},{21,5},{22,6},{23,7},{24,8},{25... | collective-permute-start | bytes 73736 | tf_op jit(solution)/shard_map/ppermute | solution.py:15
  78.7 2.7 %copy-start.5 = (bf16[1,3,3,32,32]{4,3,2,1,0:T(8,128)(2,1)S(1)}, bf16[1,3,3,32,32]{4,3,2,1,0:T(8,128)(2,1)}, u32[]{:S(2)}) copy-start(bf16[1,3,3,32,32]{4,3,2,1,0:T(8,128)(2,1)} %param.12) | copy-start | bytes 55300
  83.2 0.7 copy-start.8
